TPU v7x, 256 devices: a whole 4x4x8 slice. The times are simulated.
256 devices in a mesh: group: 4 (over z_hi), member: 64 (over y, x, z_lo, core).
Axes of the slice: x: 4, y: 4, z: 8 (z_hi: 4, z_lo: 2; z = z_hi * 2 + z_lo), core: 2. Of those that a mesh axis runs over, the one named last changes fastest.
Arguments:
- audio_vectors: bfloat16 [32768, 768], P(('group', 'member')), may hold values from -8 to 8
- sentence_vectors: bfloat16 [16384, 768], P(('group', 'member')), may hold values from -8 to 8
- matching_indices: int32 [32768], P(('group', 'member')), may hold values from 0 to 16383, as said below
- sharpness_array: float32 [1], replicated, may hold values from 8 to 16
- offset_term: float32 [1], replicated, may hold values from -4 to -2
Outputs:
- speech_grad: float32 [32768, 768], P(('group', 'member'))
- text_grad: float32 [16384, 768], P(('group', 'member'))
Inputs may be any that keep to these rules, and one draw needn't show every extreme that they name: `matching_indices`: each caption matches exactly two speech clips.
All inputs are finite; a program needn't handle non-finite values.
Results may differ from a plain program's by a relative error of at most 0.00072.
Values may be sent and summed in bfloat16 or wider, within the bound.
A program may use at most 128 MiB of HBM per device.

v0:
```python
import jax
import jax.numpy as jnp
from jax import lax
from jax.sharding import Mesh
from jax.sharding import PartitionSpec as P

MEMBER = ("member_0", "member_1", "member_2", "member_3")
GROUP_MEMBER = ("group", "member_0", "member_1", "member_2", "member_3")


def joined_along(blocks, dim):
    blocks = jnp.moveaxis(blocks, 0, dim)
    lengths = blocks.shape
    return blocks.reshape(*lengths[:dim], lengths[dim] * lengths[dim + 1], *lengths[dim + 2 :])


def copy_for_each(value, axis):
    size = lax.axis_size(axis)
    return lax.all_to_all(
        jnp.broadcast_to(value[None], (size, *value.shape)), axis, 0, 0, tiled=True
    )


def gather_directly(value, axis, dim):
    return joined_along(copy_for_each(value, axis), dim)


def split_up(value, dim, size):
    before, after = (value.shape[:dim], value.shape[dim + 1 :])
    return jnp.moveaxis(value.reshape(*before, size, -1, *after), dim, 0)


def sum_at_owner(value, axis, dim):
    size = lax.axis_size(axis)
    blocks = lax.all_to_all(split_up(value, dim, size), axis, 0, 0, tiled=True)
    return jnp.sum(blocks, axis=0)


def scatter_pairs(value, chips, core, dim):
    sizes = (lax.axis_size(chips), lax.axis_size(core))
    blocks = split_up(value, dim, sizes[0] * sizes[1])
    inside = blocks.shape[1:]
    blocks = blocks.reshape(*sizes, *inside).swapaxes(0, 1).reshape(-1, *inside)
    blocks = lax.psum_scatter(blocks, core, scatter_dimension=0, tiled=True)
    return lax.psum_scatter(blocks, chips, scatter_dimension=0, tiled=True)[0]


def unit_rows(values):
    floats = values.astype(jnp.float32)
    norms = jnp.sqrt(jnp.sum(floats * floats, axis=-1, keepdims=True) + 1e-06)
    return (floats / norms, norms)


def project_gradient(back, direction, norms):
    along = jnp.sum(direction * back, axis=-1, keepdims=True)
    return (back - direction * along) / norms


def pair_coef(audio_entries, label_rows, text_rows, columns, sharpness_factor, shift):
    logits = (
        sharpness_factor * jnp.dot(audio_entries, text_rows.T, preferred_element_type=jnp.float32)
        + shift
    )
    match = (label_rows[:, None] == columns[None, :]).astype(jnp.float32)
    return (sharpness_factor * (jax.nn.sigmoid(logits) - match)).astype(jnp.bfloat16)


def column_product(pair_weight, visitor):
    return lax.dot_general(
        pair_weight, visitor, (((0,), (0,)), ((), ())), preferred_element_type=jnp.float32
    )


def shards(audio_vectors, sentence_vectors, matching_indices, sharpness_array, offset_term):
    audio_heading, speech_norm = unit_rows(audio_vectors)
    text_dir, text_norm = unit_rows(sentence_vectors)
    speech_unit = audio_heading.astype(jnp.bfloat16)
    text_normalized = text_dir.astype(jnp.bfloat16)
    sharpness_factor = sharpness_array[0]
    shift = offset_term[0]
    group_now = lax.axis_index("group")
    text_rows = lax.all_gather(text_normalized, MEMBER, axis=0, tiled=True)
    width = text_rows.shape[0]
    columns = group_now * width + jnp.arange(width, dtype=jnp.int32)
    label_all = lax.all_gather(matching_indices, "group", axis=0, tiled=True)
    speech_all = gather_directly(speech_unit, "group", 0)
    pair_weight = pair_coef(speech_all, label_all, text_rows, columns, sharpness_factor, shift)
    speech_part = jnp.dot(pair_weight, text_rows, preferred_element_type=jnp.float32)
    speech_gradient_back = sum_at_owner(speech_part, "group", 0)
    text_part = column_product(pair_weight, speech_all)
    text_back = scatter_pairs(text_part, ("member_0", "member_1", "member_2"), "member_3", 0)
    speech_grad = project_gradient(speech_gradient_back, audio_heading, speech_norm)
    text_grad = project_gradient(text_back, text_dir, text_norm)
    return (speech_grad, text_grad)


def solution(mesh):
    split = Mesh(
        mesh.devices.reshape(mesh.shape["group"], 4, 4, 2, 2),
        ("group", "member_0", "member_1", "member_2", "member_3"),
    )
    return jax.shard_map(
        shards,
        mesh=split,
        in_specs=(P(GROUP_MEMBER, None), P(GROUP_MEMBER, None), P(GROUP_MEMBER), P(), P()),
        out_specs=(P(GROUP_MEMBER, None), P(GROUP_MEMBER, None)),
        check_vma=False,
    )
```

profile of v0, /device:TPU:64, one launch (start us, length us, event | category | flops | bytes accessed | tf_op | source)
XLA Modules:
  0.0 414.7 jit_solution(13824116031976714388)
XLA Ops:
  7.2 0.0 all-gather.3.cloned.1.call-start
  7.2 1.0 fusion.7
  8.2 1.6 fusion.10
  9.9 0.0 all-gather.3.cloned.1.call-update
  9.9 1.0 fusion.6
  11.0 1.0 fusion.11
  12.0 0.9 broadcast_in_dim.2
  12.9 8.1 %all-to-all-start = ((bf16[4,128,768]{2,1,0:T(8,128)(2,1)}), bf16[4,128,768]{2,1,0:T(8,128)(2,1)S(1)}, u32[]{:S(2)}, u32[]{:S(2)}) async-start(bf16[4,128,768]{2,1,0:T(8,128)(2,1)} %broadcast_in_dim.2), calls=%async_computation | async-start | bytes 1572864 | tf_op jit(solution)/shard_map/all_to_all | solution.py:19
  21.0 0.0 reduce-scatter.3.cloned.1.call-start
  22.3 27.0 %all-gather = s32[4,1,128]{2,1,0:T(1,128)S(1)} all-gather(s32[1,1,128]{2,1,0:T(1,128)} %bitcast.42), channel_id=1, replica_groups=mesh['group'=4,'member_0'=4,'member_1'=4,'member_2'=2,'member_3'=2] {'gr..., dimensions={0}, use_global_device_ids=true | all-gather | bytes 2560 | tf_op jit(solution)/shard_map/all_gather | solution.py:85
  49.4 0.0 all-to-all-done
  49.4 75.7 %all-gather.3.cloned.1.call-done = bf16[4096,768]{1,0:T(8,128)(2,1)} async-done(((bf16[64,768]{1,0:T(8,128)(2,1)}), bf16[4096,768]{1,0:T(8,128)(2,1)}) %all-gather.3.cloned.1.call-update) | async-done | bytes 6291472 | tf_op jit(solution)/shard_map/all_gather | solution.py:82
  125.0 10.1 %fusion.1 = (bf16[4096,512]{0,1:T(8,128)(2,1)}, f32[512,4096]{1,0:T(8,128)}) fusion(s32[4096]{0:T(1024)S(1)} %iota_add_fusion, f32[]{:T(128)} %bitcast.33, s32[512]{0:T(512)S(1)} %bitcast.40, f32[]{:T(128)} %bitcast.34, bf16[512,768]{1,0:T(8,128)(2,1)S(1)} %bitcast.38, bf16[4096,768]{1,0:T(8,128)(2,1)} %all-gather.3.cloned.1.call-done), kind=kOutput, calls=%fused_computation.2 | convolution fusion | flops 3242196992 | bytes 19679240 | tf_op jit(solution)/shard_map/dot_general | solution.py:61
  135.2 6.5 %copy.10 = bf16[4096,512]{1,0:T(8,128)(2,1)} copy(bf16[4096,512]{0,1:T(8,128)(2,1)} %get-tuple-element.2) | data formatting | bytes 8388608 | tf_op jit(solution)/shard_map/convert_element_type | solution.py:65
  141.7 10.2 %convolution_bitcast_fusion = f32[2,32,64,768]{3,2,0,1:T(8,128)} fusion(bf16[32,2,64,512]{3,2,1,0:T(8,128)(2,1)} %bitcast.36, bf16[512,768,1,1]{1,0,3,2:T(8,128)(2,1)S(1)} %bitcast.39), kind=kOutput, calls=%fused_computation.5 | convolution fusion | flops 3221225472 | bytes 17563648 | tf_op jit(solution)/shard_map/dot_general | solution.py:69
  151.9 10.5 %copy.11 = f32[2,32,64,768]{3,2,1,0:T(8,128)} copy(f32[2,32,64,768]{3,2,0,1:T(8,128)} %convolution_bitcast_fusion) | data formatting | bytes 25165824 | tf_op jit(solution)/shard_map/transpose | solution.py:43
  162.4 0.0 reduce-scatter.3.cloned.1.call-update
  162.4 0.0 reduce-scatter.5.cloned.1.call-start
  162.5 27.0 %reduce-scatter.3.cloned.1.call-done = f32[32,64,768]{2,1,0:T(8,128)} async-done(((f32[64,64,768]{2,1,0:T(8,128)}), f32[32,64,768]{2,1,0:T(8,128)}) %reduce-scatter.3.cloned.1.call-update) | async-done | bytes 6291472 | tf_op jit(solution)/shard_map/reduce_scatter | solution.py:44
  189.4 0.0 reduce-scatter.5.cloned.1.call-update
  189.5 0.0 copy-start
  189.5 0.0 copy-start.1
  189.5 8.0 %fusion.2 = f32[512,768]{1,0:T(8,128)S(1)} fusion(bf16[4096,768]{1,0:T(8,128)(2,1)} %all-gather.3.cloned.1.call-done, f32[512,4096]{1,0:T(8,128)} %get-tuple-element.3, s32[4096]{0:T(1024)S(1)} %iota_add_fusion, f32[]{:T(128)} %bitcast.32, s32[512]{0:T(512)S(1)} %bitcast.41), kind=kOutput, calls=%fused_computation.6 | convolution fusion | flops 3231711232 | bytes 16271364 | tf_op jit(solution)/shard_map/dot_general | solution.py:88
  197.5 60.5 %all_to_all.10 = f32[4,128,768]{2,1,0:T(8,128)S(1)} all-to-all(f32[4,128,768]{2,1,0:T(8,128)S(1)} %bitcast.37), channel_id=1, replica_groups=mesh['group'=4,'member_0'=4,'member_1'=4,'member_2'=2,'member_3'=2] {'gr..., dimensions={0} | all-to-all | bytes 3145728 | tf_op jit(solution)/shard_map/all_to_all | solution.py:35
  258.0 0.1 reduce_sum.47
  258.1 0.0 copy-done
  258.1 0.2 multiply_reduce_fusion
  258.3 0.9 subtract_divide_fusion
  259.2 146.1 %reduce-scatter.5.cloned.1.call-done = f32[1,64,768]{2,1,0:T(8,128)} async-done(((f32[32,64,768]{2,1,0:T(8,128)}), f32[1,64,768]{2,1,0:T(8,128)}) %reduce-scatter.5.cloned.1.call-update) | async-done | bytes 196624 | tf_op jit(solution)/shard_map/reduce_scatter | solution.py:45
  405.4 0.0 copy-done.1
  405.4 1.1 fusion.8
  406.5 1.7 fusion.9
  (3 shorter events, 0.0 us)
Async XLA Ops:
  7.2 117.9 %all-gather.3.cloned.1.call-start = ((), (), s32[]{:S(2)}) async-start(), calls=%async_computation.4 | async-start | bytes 6389760 | tf_op jit(solution)/shard_map/all_gather | solution.py:82
  12.9 36.4 %all-to-all-start = ((bf16[4,128,768]{2,1,0:T(8,128)(2,1)}), bf16[4,128,768]{2,1,0:T(8,128)(2,1)S(1)}, u32[]{:S(2)}, u32[]{:S(2)}) async-start(bf16[4,128,768]{2,1,0:T(8,128)(2,1)} %broadcast_in_dim.2), calls=%async_computation | async-start | bytes 1572864 | tf_op jit(solution)/shard_map/all_to_all | solution.py:19
  21.0 168.4 %reduce-scatter.3.cloned.1.call-start = ((), (), s32[]{:S(2)}) async-start(), calls=%async_computation.5 | async-start | bytes 18874368 | tf_op jit(solution)/shard_map/reduce_scatter | solution.py:44
  162.4 242.9 %reduce-scatter.5.cloned.1.call-start = ((), (), s32[]{:S(2)}) async-start(), calls=%async_computation.6 | async-start | bytes 6488064 | tf_op jit(solution)/shard_map/reduce_scatter | solution.py:45
  189.5 68.7 %copy-start = (bf16[128,768]{1,0:T(8,128)(2,1)S(1)}, bf16[128,768]{1,0:T(8,128)(2,1)}, u32[]{:S(2)}) copy-start(bf16[128,768]{1,0:T(8,128)(2,1)} %param.5) | copy-start | bytes 589828
  189.5 215.9 %copy-start.1 = (bf16[64,768]{1,0:T(8,128)(2,1)S(1)}, bf16[64,768]{1,0:T(8,128)(2,1)}, u32[]{:S(2)}) copy-start(bf16[64,768]{1,0:T(8,128)(2,1)} %param.6) | copy-start | bytes 294916
Sparse Core Ops, SparseCore 0:
  10.4 114.5 all-gather.2
  162.5 26.8 reduce-scatter.2
  192.0 213.3 reduce-scatter.4
where the time goes:
time: 415 us
  waiting for transfers between devices  249 us (60%)
  blocking collectives  87.5 us (21%)
  matrix products  28.3 us (7%)
  local copies, waits for them, and re-layouts  18 us (4%)
  between operations  15.1 us (4%)
  other arithmetic  8.8 us (2%)
  starting transfers between devices  8.19 us (2%)
    reduce_scatter x1, waiting for transfers between devices, scatter_pairs(): return lax.psum_scatter(blocks, chips, scatter_dimension=0, tiled=True)[0]  146 us
    all_gather x1, waiting for transfers between devices, shards(): text_rows = lax.all_gather(text_normalized, MEMBER, axis=0, tiled=True)  75.7 us
    all_to_all x1, blocking collectives, sum_at_owner(): blocks = lax.all_to_all(split_up(value, dim, size), axis, 0, 0, tiled=True)  60.5 us
    all_gather x1, blocking collectives, shards(): label_all = lax.all_gather(matching_indices, 'group', axis=0, tiled=True)  27 us
    reduce_scatter x1, waiting for transfers between devices, scatter_pairs(): blocks = lax.psum_scatter(blocks, core, scatter_dimension=0, tiled=True)  27 us
    transpose x1, local copies, waits for them, and re-layouts, scatter_pairs(): blocks = blocks.reshape(*sizes, *inside).swapaxes(0, 1).reshape(-1, *inside)  10.5 us
    dot_general x1, matrix products, column_product(): lax.dot_general(pair_weight, visitor, (((0,), (0,)), ((), ())), preferred...  10.2 us
    dot_general x1, matrix products, pair_coef(): jnp.dot(audio_entries, text_rows.T, preferred_element_type=jnp.float32)  10.1 us
  transfers between devices with their start and end apart: 4, of which 3 were waited for; matrix products, arithmetic and copies ran while one was open for 3% of the time, Pallas kernels for 0%

commit v1 on v0

--- a/solution.py
+++ b/solution.py
@@ -82,7 +82,10 @@
     text_rows = lax.all_gather(text_normalized, MEMBER, axis=0, tiled=True)
     width = text_rows.shape[0]
     columns = group_now * width + jnp.arange(width, dtype=jnp.int32)
-    label_all = lax.all_gather(matching_indices, "group", axis=0, tiled=True)
+    label_all = jnp.concatenate(
+        lax.all_to_all(jnp.stack([matching_indices] * lax.axis_size("group")), "group", 0, 0),
+        axis=0,
+    )
     speech_all = gather_directly(speech_unit, "group", 0)
     pair_weight = pair_coef(speech_all, label_all, text_rows, columns, sharpness_factor, shift)
     speech_part = jnp.dot(pair_weight, text_rows, preferred_element_type=jnp.float32)

time: 415 us -> 416 us (level)
  blocking collectives: 87.5 us -> 60.7 us
  waiting for transfers between devices: 249 us -> 270 us
  starting transfers between devices: 8.19 us -> 14 us
    all_gather x1 -> x0, blocking collectives: 27 us -> none  [shards(): label_all = lax.all_gather(matching_indices, 'group', axis=0, tiled=True)]
    all_to_all x1, waiting for transfers between devices: 0.01 us -> 25.1 us  [copy_for_each(): lax.all_to_all(jnp.broadcast_to(value[None], (size, *value.shape)), axis,...]
    all_to_all x0 -> x1, starting transfers between devices: none -> 8.11 us  [shards(): lax.all_to_all(jnp.stack([matching_indices] * lax.axis_size('group')), 'g...]
    all_gather x1, waiting for transfers between devices: 75.7 us -> 69.2 us  [shards(): text_rows = lax.all_gather(text_normalized, MEMBER, axis=0, tiled=True)]
  transfers between devices with their start and end apart: 4 -> 5, of which waited for: 3 -> 5; matrix products, arithmetic and copies ran while one was open for 3% -> 3% of each run, Pallas kernels for 0% -> 0%
where the time goes in v1:
time: 416 us
  waiting for transfers between devices  270 us (65%)
  blocking collectives  60.7 us (15%)
  matrix products  28.4 us (7%)
  local copies, waits for them, and re-layouts  19.2 us (5%)
  between operations  15.1 us (4%)
  starting transfers between devices  14 us (3%)
  other arithmetic  8.8 us (2%)
    reduce_scatter x1, waiting for transfers between devices, scatter_pairs(): return lax.psum_scatter(blocks, chips, scatter_dimension=0, tiled=True)[0]  146 us
    all_gather x1, waiting for transfers between devices, shards(): text_rows = lax.all_gather(text_normalized, MEMBER, axis=0, tiled=True)  69.2 us
    all_to_all x1, blocking collectives, sum_at_owner(): blocks = lax.all_to_all(split_up(value, dim, size), axis, 0, 0, tiled=True)  60.7 us
    reduce_scatter x1, waiting for transfers between devices, scatter_pairs(): blocks = lax.psum_scatter(blocks, core, scatter_dimension=0, tiled=True)  25.7 us
    all_to_all x1, waiting for transfers between devices, copy_for_each(): lax.all_to_all(jnp.broadcast_to(value[None], (size, *value.shape)), axis,...  25.1 us
    transpose x1, local copies, waits for them, and re-layouts, scatter_pairs(): blocks = blocks.reshape(*sizes, *inside).swapaxes(0, 1).reshape(-1, *inside)  10.5 us
    dot_general x1, matrix products, column_product(): lax.dot_general(pair_weight, visitor, (((0,), (0,)), ((), ())), preferred...  10.2 us
    dot_general x1, matrix products, pair_coef(): jnp.dot(audio_entries, text_rows.T, preferred_element_type=jnp.float32)  10.1 us
  transfers between devices with their start and end apart: 5, of which 5 were waited for; matrix products, arithmetic and copies ran while one was open for 3% of the time, Pallas kernels for 0%

profile of v1, /device:TPU:64, one launch (start us, length us, event | category | flops | bytes accessed | tf_op | source)
XLA Modules:
  0.0 415.8 jit_solution(9708500684130878948)
XLA Ops:
  7.2 0.0 all-gather.2.cloned.1.call-start
  7.2 1.0 fusion.7
  8.2 1.6 fusion.10
  9.9 0.0 all-gather.2.cloned.1.call-update
  9.9 1.2 stack.2
  11.1 8.1 %all-to-all-start.1 = ((s32[4,1,128]{2,1,0:T(1,128)}), s32[4,1,128]{2,1,0:T(1,128)S(1)}, u32[]{:S(2)}, u32[]{:S(2)}) async-start(s32[4,1,128]{2,1,0:T(1,128)} %stack.2), calls=%async_computation.1 | async-start | bytes 4096 | tf_op jit(solution)/shard_map/all_to_all | solution.py:86
  19.2 1.0 fusion.6
  20.3 1.0 fusion.11
  21.3 3.2 all-to-all-done.1
  24.5 0.9 broadcast_in_dim.2
  25.4 5.8 %all-to-all-start = ((bf16[4,128,768]{2,1,0:T(8,128)(2,1)}), bf16[4,128,768]{2,1,0:T(8,128)(2,1)S(1)}, u32[]{:S(2)}, u32[]{:S(2)}) async-start(bf16[4,128,768]{2,1,0:T(8,128)(2,1)} %broadcast_in_dim.2), calls=%async_computation | async-start | bytes 1572864 | tf_op jit(solution)/shard_map/all_to_all | solution.py:19
  31.2 0.0 reduce-scatter.3.cloned.1.call-start
  32.6 25.1 %all-to-all-done = bf16[4,128,768]{2,1,0:T(8,128)(2,1)S(1)} async-done(((bf16[4,128,768]{2,1,0:T(8,128)(2,1)}), bf16[4,128,768]{2,1,0:T(8,128)(2,1)S(1)}, u32[]{:S(2)}, u32[]{:S(2)}) %all-to-all-start) | async-done | bytes 786464 | tf_op jit(solution)/shard_map/all_to_all | solution.py:19
  57.7 69.2 %all-gather.2.cloned.1.call-done = bf16[4096,768]{1,0:T(8,128)(2,1)} async-done(((bf16[64,768]{1,0:T(8,128)(2,1)}), bf16[4096,768]{1,0:T(8,128)(2,1)}) %all-gather.2.cloned.1.call-update) | async-done | bytes 6291472 | tf_op jit(solution)/shard_map/all_gather | solution.py:82
  126.9 10.1 %fusion.1 = (bf16[4096,512]{0,1:T(8,128)(2,1)}, f32[512,4096]{1,0:T(8,128)}) fusion(s32[4096]{0:T(1024)S(1)} %iota_add_fusion, f32[]{:T(128)} %bitcast.32, s32[512]{0:T(512)S(1)} %bitcast.39, f32[]{:T(128)} %bitcast.33, bf16[512,768]{1,0:T(8,128)(2,1)S(1)} %bitcast.37, bf16[4096,768]{1,0:T(8,128)(2,1)} %all-gather.2.cloned.1.call-done), kind=kOutput, calls=%fused_computation.2 | convolution fusion | flops 3242196992 | bytes 19679240 | tf_op jit(solution)/shard_map/dot_general | solution.py:61
  137.0 6.5 %copy.8 = bf16[4096,512]{1,0:T(8,128)(2,1)} copy(bf16[4096,512]{0,1:T(8,128)(2,1)} %get-tuple-element.2) | data formatting | bytes 8388608 | tf_op jit(solution)/shard_map/convert_element_type | solution.py:65
  143.5 10.2 %convolution_bitcast_fusion = f32[2,32,64,768]{3,2,0,1:T(8,128)} fusion(bf16[32,2,64,512]{3,2,1,0:T(8,128)(2,1)} %bitcast.35, bf16[512,768,1,1]{1,0,3,2:T(8,128)(2,1)S(1)} %bitcast.38), kind=kOutput, calls=%fused_computation.5 | convolution fusion | flops 3221225472 | bytes 17563648 | tf_op jit(solution)/shard_map/dot_general | solution.py:69
  153.7 10.5 %copy.9 = f32[2,32,64,768]{3,2,1,0:T(8,128)} copy(f32[2,32,64,768]{3,2,0,1:T(8,128)} %convolution_bitcast_fusion) | data formatting | bytes 25165824 | tf_op jit(solution)/shard_map/transpose | solution.py:43
  164.3 0.0 reduce-scatter.3.cloned.1.call-update
  164.3 0.0 reduce-scatter.5.cloned.1.call-start
  164.3 25.7 %reduce-scatter.3.cloned.1.call-done = f32[32,64,768]{2,1,0:T(8,128)} async-done(((f32[64,64,768]{2,1,0:T(8,128)}), f32[32,64,768]{2,1,0:T(8,128)}) %reduce-scatter.3.cloned.1.call-update) | async-done | bytes 6291472 | tf_op jit(solution)/shard_map/reduce_scatter | solution.py:44
  190.0 0.0 reduce-scatter.5.cloned.1.call-update
  190.1 0.0 copy-start
  190.1 0.0 copy-start.1
  190.1 8.0 %fusion.2 = f32[512,768]{1,0:T(8,128)S(1)} fusion(bf16[4096,768]{1,0:T(8,128)(2,1)} %all-gather.2.cloned.1.call-done, f32[512,4096]{1,0:T(8,128)} %get-tuple-element.3, s32[4096]{0:T(1024)S(1)} %iota_add_fusion, f32[]{:T(128)} %bitcast.31, s32[512]{0:T(512)S(1)} %bitcast.40), kind=kOutput, calls=%fused_computation.6 | convolution fusion | flops 3231711232 | bytes 16271364 | tf_op jit(solution)/shard_map/dot_general | solution.py:91
  198.1 60.7 %all_to_all.16 = f32[4,128,768]{2,1,0:T(8,128)S(1)} all-to-all(f32[4,128,768]{2,1,0:T(8,128)S(1)} %bitcast.36), channel_id=1, replica_groups=mesh['group'=4,'member_0'=4,'member_1'=4,'member_2'=2,'member_3'=2] {'gr..., dimensions={0} | all-to-all | bytes 3145728 | tf_op jit(solution)/shard_map/all_to_all | solution.py:35
  258.8 0.1 reduce_sum.47
  259.0 0.0 copy-done
  259.0 0.2 multiply_reduce_fusion
  259.2 0.9 subtract_divide_fusion
  260.1 146.4 %reduce-scatter.5.cloned.1.call-done = f32[1,64,768]{2,1,0:T(8,128)} async-done(((f32[32,64,768]{2,1,0:T(8,128)}), f32[1,64,768]{2,1,0:T(8,128)}) %reduce-scatter.5.cloned.1.call-update) | async-done | bytes 196624 | tf_op jit(solution)/shard_map/reduce_scatter | solution.py:45
  406.4 0.0 copy-done.1
  406.4 1.1 fusion.8
  407.6 1.7 fusion.9
  (3 shorter events, 0.0 us)
Async XLA Ops:
  7.2 119.7 %all-gather.2.cloned.1.call-start = ((), (), s32[]{:S(2)}) async-start(), calls=%async_computation.5 | async-start | bytes 6389760 | tf_op jit(solution)/shard_map/all_gather | solution.py:82
  11.1 13.4 %all-to-all-start.1 = ((s32[4,1,128]{2,1,0:T(1,128)}), s32[4,1,128]{2,1,0:T(1,128)S(1)}, u32[]{:S(2)}, u32[]{:S(2)}) async-start(s32[4,1,128]{2,1,0:T(1,128)} %stack.2), calls=%async_computation.1 | async-start | bytes 4096 | tf_op jit(solution)/shard_map/all_to_all | solution.py:86
  25.4 32.3 %all-to-all-start = ((bf16[4,128,768]{2,1,0:T(8,128)(2,1)}), bf16[4,128,768]{2,1,0:T(8,128)(2,1)S(1)}, u32[]{:S(2)}, u32[]{:S(2)}) async-start(bf16[4,128,768]{2,1,0:T(8,128)(2,1)} %broadcast_in_dim.2), calls=%async_computation | async-start | bytes 1572864 | tf_op jit(solution)/shard_map/all_to_all | solution.py:19
  31.2 158.8 %reduce-scatter.3.cloned.1.call-start = ((), (), s32[]{:S(2)}) async-start(), calls=%async_computation.6 | async-start | bytes 18874368 | tf_op jit(solution)/shard_map/reduce_scatter | solution.py:44
  164.3 242.2 %reduce-scatter.5.cloned.1.call-start = ((), (), s32[]{:S(2)}) async-start(), calls=%async_computation.7 | async-start | bytes 6488064 | tf_op jit(solution)/shard_map/reduce_scatter | solution.py:45
  190.1 68.9 %copy-start = (bf16[128,768]{1,0:T(8,128)(2,1)S(1)}, bf16[128,768]{1,0:T(8,128)(2,1)}, u32[]{:S(2)}) copy-start(bf16[128,768]{1,0:T(8,128)(2,1)} %param.5) | copy-start | bytes 589828
  190.1 216.4 %copy-start.1 = (bf16[64,768]{1,0:T(8,128)(2,1)S(1)}, bf16[64,768]{1,0:T(8,128)(2,1)}, u32[]{:S(2)}) copy-start(bf16[64,768]{1,0:T(8,128)(2,1)} %param.6) | copy-start | bytes 294916
Sparse Core Ops, SparseCore 0:
  10.4 116.4 all-gather.1
  164.4 25.5 reduce-scatter.2
  192.6 213.7 reduce-scatter.4
